TPU v7x, 1024 devices: a whole 4x8x16 slice. The times are simulated.
1024 devices in a mesh: gx: 8 (over y), gy: 4 (over x), gz: 32 (over z, core).
Axes of the slice: x: 4, y: 8, z: 16, core: 2. Of those that a mesh axis runs over, the one named last changes fastest.
Arguments:
- rhs: float32 [8, 4, 32, 2, 64, 256], P('gx', 'gy', 'gz'), may hold values from -6 to 6
- viscosity: float32 [8, 4, 32, 64], P('gx', 'gy', 'gz'), may hold values from 0.3 to 3
- counts: int32 [8, 4, 32], P('gx', 'gy', 'gz'), may hold values from 8 to 64, as said below
- neighbours: int32 [8, 4, 32, 16], P('gx', 'gy', 'gz'), may hold values from -1 to 31, as said below
- face_index: int32 [8, 4, 32, 16, 512], P('gx', 'gy', 'gz'), may hold values from 0 to 16383, as said below
- k_matrix: float32 [256, 256], replicated, may hold values from -0.04 to 1.04, as said below
- p_matrix: float32 [256, 256], replicated, may hold values from -0.04 to 1.04, as said below
Outputs:
- solution: float32 [8, 4, 32, 2, 64, 256], P('gx', 'gy', 'gz')
Inputs may be any that keep to these rules, and one draw needn't show every extreme that they name: `counts`: in every gz group some partition has exactly 64 live elements. `neighbours`: each list names distinct partitions of the same gz group in increasing order, followed by -1 entries; the relation is symmetric and no partition names itself. `face_index`: every index lies within the live elements of its partition, that is below 256 times counts. `k_matrix`: the identity plus independent entries. `p_matrix`: the identity plus independent entries.
All inputs are finite; a program needn't handle non-finite values.
Results may differ from a plain program's by a relative error of at most 0.0003.
Values sent between devices are 32-bit elements; how exact they have to be, the bound alone decides.
A program may use at most 32 MiB of HBM per device.

v0:
```python
import jax
import jax.numpy as jnp
from jax import lax
from jax.sharding import PartitionSpec as P

coupling = 0.5
largest_rank = lax.Precision.HIGHEST


def per_element(vector, matrix):
    shaped = vector.shape
    product = jnp.dot(
        vector.reshape(-1, shaped[-1]),
        matrix,
        precision=largest_rank,
        preferred_element_type=jnp.float32,
    )
    return product.reshape(shaped)


def shared_faces(departing_rows, links, probes, slots, width):
    flat_rows = departing_rows.reshape(slots, probes * width)
    my_index = lax.axis_index("gz")
    face_vals = lax.all_gather(flat_rows[None], "gz", axis=0, tiled=True)
    link_rows = lax.all_gather(links[None], "gz", axis=0, tiled=True)
    count_src = link_rows.shape[0]
    sources = jnp.arange(count_src, dtype=jnp.int32)
    pick_rows = (links[:, None] == sources[None, :]).astype(jnp.float32)
    to_self = (link_rows == my_index).astype(jnp.float32)
    selection = (pick_rows[:, :, None] * to_self[None, :, :]).reshape(slots, count_src * slots)
    gathered_rows = face_vals.reshape(count_src * slots, probes * width)
    return jnp.dot(
        selection, gathered_rows, precision=largest_rank, preferred_element_type=jnp.float32
    )


def operate(vector, k_matrix, visc_col, live_mask, links, blocks):
    probes, elements, dofs = vector.shape
    slots, width = blocks.shape
    flat_vec = vector.reshape(probes, elements * dofs)
    flat_index = blocks.reshape(-1)
    departing_rows = flat_vec[:, flat_index].reshape(probes, slots, width).transpose(1, 0, 2)
    received_rows = shared_faces(departing_rows, links, probes, slots, width)
    received_rows = (
        received_rows.reshape(slots, probes, width).transpose(1, 0, 2).reshape(probes, -1)
    )
    placed = jnp.zeros((probes, elements * dofs), jnp.float32).at[:, flat_index].add(received_rows)
    return (
        per_element(vector, k_matrix) * visc_col - coupling * placed.reshape(vector.shape)
    ) * live_mask


def inner_prod(left_vec, right_vec):
    return jnp.sum(left_vec * right_vec, axis=(1, 2))


def per_device(rhs, viscosity, counts, neighbours, face_index, k_matrix, p_matrix):
    vector = rhs[0, 0, 0]
    elements = vector.shape[1]
    live_count = counts[0, 0, 0]
    live_mask = (jnp.arange(elements, dtype=jnp.int32) < live_count).astype(jnp.float32)[
        None, :, None
    ]
    visc_col = viscosity[0, 0, 0][None, :, None]
    links = neighbours[0, 0, 0]
    blocks = face_index[0, 0, 0]
    source = vector * live_mask

    def smooth(field_in):
        return per_element(field_in, p_matrix) / visc_col * live_mask

    def apply_op(field_in):
        return operate(field_in, k_matrix, visc_col, live_mask, links, blocks)

    search_raw = smooth(source)
    image_raw = apply_op(search_raw)
    rhs_square, cross_raw, image_square = lax.psum(
        (
            inner_prod(source, source),
            inner_prod(source, image_raw),
            inner_prod(image_raw, image_raw),
        ),
        ("gx", "gy", "gz"),
    )
    rhs_length = jnp.sqrt(rhs_square)
    basis_one = source / rhs_length[:, None, None]
    search_one = search_raw / rhs_length[:, None, None]
    image_one = image_raw / rhs_length[:, None, None]
    top_one = cross_raw / rhs_square
    first_square = image_square / rhs_square
    below_one = jnp.sqrt(first_square - top_one * top_one)
    basis_two = (image_one - top_one[:, None, None] * basis_one) / below_one[:, None, None]
    search_two = smooth(basis_two)
    image_two = apply_op(search_two)
    top_two, middle_two, square_two = lax.psum(
        (
            inner_prod(basis_one, image_two),
            inner_prod(basis_two, image_two),
            inner_prod(image_two, image_two),
        ),
        ("gx", "gy", "gz"),
    )
    cross_term = top_one * top_two + below_one * middle_two
    determinant = first_square * square_two - cross_term * cross_term
    weight_one = rhs_length * (square_two * top_one - cross_term * top_two) / determinant
    weight_two = rhs_length * (first_square * top_two - cross_term * top_one) / determinant
    solution = weight_one[:, None, None] * search_one + weight_two[:, None, None] * search_two
    return solution[None, None, None]


def solution(mesh):
    return jax.shard_map(
        per_device,
        mesh=mesh,
        in_specs=(
            P("gx", "gy", "gz", None, None, None),
            P("gx", "gy", "gz", None),
            P("gx", "gy", "gz"),
            P("gx", "gy", "gz", None),
            P("gx", "gy", "gz", None, None),
            P(),
            P(),
        ),
        out_specs=P("gx", "gy", "gz", None, None, None),
        check_vma=False,
    )
```

profile of v0, /device:TPU:1, one launch (start us, length us, event | category | flops | bytes accessed | tf_op | source)
XLA Modules:
  0.0 622.4 jit_solution(4844925450892302290)
XLA Ops:
  8.1 1.2 fusion.9
  9.3 4.6 copy.44
  14.0 31.1 %gather_fusion = f32[8192,2]{1,0:T(8,128)} fusion(f32[2,16384]{0,1:T(8,128)} %bitcast.81, s32[8192]{0:T(1024)S(1)} %broadcast_clamp_fusion), kind=kCustom, calls=%fused_computation | custom fusion | bytes 163840 | tf_op jit(solution)/shard_map/gather | solution.py:42
  45.1 2.8 copy.35
  48.7 44.4 %all-gather = s32[32,1,1,16]{3,2,1,0:T(1,128)S(1)} all-gather(s32[1,1,1,16]{3,2,1,0:T(1,128)S(1)} %copy-done.4), channel_id=2, replica_groups=mesh['gx'=8,'gy'=4,'gz'=32] {'gz'}, dimensions={0}, use_global_device_ids=true | all-gather | bytes 2112 | tf_op jit(solution)/shard_map/all_gather | solution.py:25
  93.5 39.5 %all-gather.4.cloned.1.call-done = f32[32,16,1024]{2,1,0:T(8,128)} async-done(((f32[1,16,1024]{2,1,0:T(8,128)}), f32[32,16,1024]{2,1,0:T(8,128)}) %all-gather.4.cloned.1.call-update) | async-done | bytes 2097168 | tf_op jit(solution)/shard_map/all_gather | solution.py:24
  133.0 1.9 copy.36
  134.9 1.8 convolution_bitcast_fusion.1
  136.7 2.6 copy.45
  139.4 48.0 %scatter_custom_fusion = f32[2,16384]{0,1:T(8,128)} fusion(s32[8192]{0:T(1024)S(1)} %bitcast.95, f32[8192,2]{1,0:T(8,128)} %bitcast.87, f32[]{:T(128)} %constant.5.clone.1), kind=kCustom, calls=%fused_computation.8 | custom fusion | flops 16384 | bytes 131584 | tf_op jit(solution)/shard_map/scatter-add | solution.py:47
  187.4 5.7 broadcast_multiply_fusion.1
  193.1 5.4 copy.51
  198.9 121.7 %all-reduce.1 = (f32[2]{0:T(128)S(1)}, f32[2]{0:T(128)S(1)}, f32[2]{0:T(128)S(1)}) all-reduce(f32[2]{0:T(128)S(1)} %get-tuple-element.10, f32[2]{0:T(128)S(1)} %get-tuple-element.6, f32[2]{0:T(128)S(1)} %get-tuple-element.5), channel_id=1, replica_groups=mesh['gx'=8,'gy'=4,'gz'=32] {'gx','gy','gz'}, use_global_device_ids=true, to_apply=%region_6.0 | all-reduce | flops 6 | bytes 48 | tf_op jit(solution)/shard_map/psum | solution.py:77
  321.1 4.6 copy.46
  325.7 31.1 %gather_fusion.1 = f32[8192,2]{1,0:T(8,128)} fusion(f32[2,16384]{0,1:T(8,128)} %bitcast.80, s32[8192]{0:T(1024)S(1)} %broadcast_clamp_fusion), kind=kCustom, calls=%fused_computation.1 | custom fusion | bytes 163840 | tf_op jit(solution)/shard_map/gather | solution.py:42
  356.8 2.8 copy.40
  360.4 67.0 %all-gather.6.cloned.1.call-done = f32[32,16,1024]{2,1,0:T(8,128)} async-done(((f32[1,16,1024]{2,1,0:T(8,128)}), f32[32,16,1024]{2,1,0:T(8,128)}) %all-gather.6.cloned.1.call-update) | async-done | bytes 2097168 | tf_op jit(solution)/shard_map/all_gather | solution.py:24
  427.3 1.9 copy.41
  429.3 1.8 convolution_bitcast_fusion
  431.1 2.6 copy.47
  433.7 48.0 %scatter_custom_fusion.1 = f32[2,16384]{0,1:T(8,128)} fusion(s32[8192]{0:T(1024)S(1)} %bitcast.96, f32[8192,2]{1,0:T(8,128)} %bitcast.86, f32[]{:T(128)} %constant.5.clone.1), kind=kCustom, calls=%fused_computation.6 | custom fusion | flops 16384 | bytes 131584 | tf_op jit(solution)/shard_map/scatter-add | solution.py:47
  481.7 5.7 broadcast_multiply_fusion
  487.5 5.3 copy.52
  493.2 121.5 %all-reduce = (f32[2]{0:T(128)S(1)}, f32[2]{0:T(128)S(1)}, f32[2]{0:T(128)S(1)}) all-reduce(f32[2]{0:T(128)S(1)} %get-tuple-element.8, f32[2]{0:T(128)S(1)} %get-tuple-element.9, f32[2]{0:T(128)S(1)} %get-tuple-element.7), channel_id=1, replica_groups=mesh['gx'=8,'gy'=4,'gz'=32] {'gx','gy','gz'}, use_global_device_ids=true, to_apply=%region_11.0 | all-reduce | flops 6 | bytes 48 | tf_op jit(solution)/shard_map/psum | solution.py:95
  (33 shorter events, 4.7 us)
Async XLA Ops:
  6.5 1.6 copy-start
  6.5 42.2 %copy-start.4 = (s32[1,1,1,16]{3,2,1,0:T(1,128)S(1)}, s32[1,1,1,16]{3,2,1,0:T(1,128)}, u32[]{:S(2)}) copy-start(s32[1,1,1,16]{3,2,1,0:T(1,128)} %param.10) | copy-start | bytes 196
  6.5 126.5 %all-gather.4.cloned.1.call-start = ((), (), s32[]{:S(2)}) async-start(), calls=%async_computation | async-start | bytes 2162688 | tf_op jit(solution)/shard_map/all_gather | solution.py:24
  48.6 378.7 %all-gather.6.cloned.1.call-start = ((), (), s32[]{:S(2)}) async-start(), calls=%async_computation.1 | async-start | bytes 2162688 | tf_op jit(solution)/shard_map/all_gather | solution.py:24
  193.1 5.4 copy-start.2
  193.1 5.4 copy-start.3
  193.1 5.4 copy-start.5
  481.7 133.8 %copy-start.1 = (f32[256,256]{1,0:T(8,128)S(1)}, f32[256,256]{1,0:T(8,128)}, u32[]{:S(2)}) copy-start(f32[256,256]{1,0:T(8,128)} %param.13) | copy-start | bytes 786436
Sparse Core Ops, SparseCore 0:
  48.8 84.1 all-gather.3
  360.5 66.7 all-gather.5
where the time goes:
time: 623 us; the launch traced here: 622 us
  blocking collectives  288 us (46%)
  other arithmetic  109 us (17%)
  waiting for transfers between devices  106 us (17%)
  local copies, waits for them, and re-layouts  99.4 us (16%)
  between operations  14.3 us (2%)
    psum x1, blocking collectives, per_device(): lax.psum((inner_prod(source, source), inner_prod(source, image_raw), inne...  122 us
    psum x1, blocking collectives, per_device(): lax.psum((inner_prod(basis_one, image_two), inner_prod(basis_two, image_t...  122 us
    all_gather x2, waiting for transfers between devices, shared_faces(): face_vals = lax.all_gather(flat_rows[None], 'gz', axis=0, tiled=True)  106 us
    scatter-add x2, other arithmetic, operate(): jnp.zeros((probes, elements * dofs), jnp.float32).at[:, flat_index]  96 us
    gather x2, local copies, waits for them, and re-layouts, operate(): flat_vec[:, flat_index].reshape(probes, slots, width).transpose(1, 0, 2)  62.2 us
    all_gather x1, blocking collectives, shared_faces(): link_rows = lax.all_gather(links[None], 'gz', axis=0, tiled=True)  44.4 us
  transfers between devices with their start and end apart: 2, of which 2 were waited for; matrix products, arithmetic and copies ran while one was open for 0% of the time, Pallas kernels for 0%

commit v1 on v0

v1 whole, which is shorter than its diff:
```python
import functools

import jax
import jax.numpy as jnp
from jax import lax
from jax.experimental import pallas as pl
from jax.experimental.pallas import tpu as pltpu
from jax.sharding import PartitionSpec as P

MESH = pl.DeviceIdType.MESH
coupling = 0.5
LANES = 128
f32 = jnp.float32
bf16 = jnp.bfloat16


def halves(x):
    high = x.astype(bf16)
    low = (x - high.astype(f32)).astype(bf16)
    return high, low


def nn_dot(a, b):
    return lax.dot_general(a, b, (((1,), (0,)), ((), ())), preferred_element_type=f32)


def nt_dot(a, b):
    return lax.dot_general(a, b, (((1,), (1,)), ((), ())), preferred_element_type=f32)


def kernel(
    nx, ny, nz, slots, probes, elements, dofs, width,
    rhs_hbm, visc_hbm, counts_hbm, links_hbm, index_hbm, k_hbm, p_hbm,
    out_ref,
    rhs, visc, counts, links, index, k_raw, p_raw,
    k_high, k_low, p_high, p_low, onehot, faces, departing, arriving_a, arriving_b, placed,
    sums_z, sums_xy, load_sems, send_sems, recv_sems,
):
    ix, iy, me = lax.axis_index("gx"), lax.axis_index("gy"), lax.axis_index("gz")
    nxy = nx * ny
    plane = ix * ny + iy
    rows = probes * elements
    pieces = width // LANES

    def z_peer(j):
        half = nz // 2
        offset = half + ((j + 1) // 2) * (1 - 2 * (j % 2))
        return lax.rem(me + offset, nz)

    def xy_peer(j):
        return lax.rem(plane + 1 + j, nxy)

    barrier = pltpu.get_barrier_semaphore()

    def greet_z(j, carry):
        pl.semaphore_signal(barrier, inc=1, device_id=(ix, iy, z_peer(j)), device_id_type=MESH)
        return carry

    def greet_xy(j, carry):
        other = xy_peer(j)
        pl.semaphore_signal(barrier, inc=1, device_id=(other // ny, other % ny, me), device_id_type=MESH)
        return carry

    loads = [
        pltpu.make_async_copy(src, dst, load_sems.at[i])
        for i, (src, dst) in enumerate(
            (
                (index_hbm, index), (rhs_hbm, rhs), (p_hbm, p_raw), (visc_hbm, visc),
                (counts_hbm, counts), (links_hbm, links), (k_hbm, k_raw),
            )
        )
    ]
    for load in loads:
        load.start()
    lax.fori_loop(0, nz - 1, greet_z, 0)
    lax.fori_loop(0, nxy - 1, greet_xy, 0)

    loads[3].wait()
    loads[4].wait()
    loads[5].wait()
    element_id = lax.broadcasted_iota(jnp.int32, (elements, 1), 0)
    live = (element_id < counts[0:1, 0:1]).astype(f32)
    diagonal = lax.broadcasted_iota(jnp.int32, (elements, elements), 0) == lax.broadcasted_iota(
        jnp.int32, (elements, elements), 1
    )
    visc_col = jnp.sum(jnp.where(diagonal, visc[0:1, :], 0.0), axis=1, keepdims=True)
    live_rows = jnp.concatenate([live] * probes, axis=0)
    visc_rows = jnp.concatenate([visc_col] * probes, axis=0)
    inverse_rows = live_rows / visc_rows

    loads[1].wait()
    loads[2].wait()
    p_high[...], p_low[...] = halves(p_raw[...])
    source = jnp.where(live_rows > 0.0, rhs[...], 0.0)

    def per_element(x, m_high, m_low):
        high, low = halves(x)
        both = nn_dot(jnp.concatenate([high, low], axis=0), m_high[...])
        return both[:rows] + both[rows:] + nn_dot(high, m_low[...])

    link_of = [jnp.broadcast_to(links[0:1, l : l + 1], (8, LANES)) for l in range(slots)]

    def gather(x, first):
        stacked = jnp.concatenate(halves(x), axis=0)

        def one_slot(l, carry):
            where_to = index[pl.ds(l, 1), :]
            if first:
                dof = where_to % dofs if dofs & (dofs - 1) else where_to & (dofs - 1)
                ids = lax.broadcasted_iota(jnp.int32, (dofs, width), 0)
                hot = jnp.where(dof == ids, 1.0, 0.0).astype(bf16)
                onehot[l] = hot
            else:
                hot = onehot[l]
            spread = nn_dot(stacked, hot)
            spread = spread[:rows] + spread[rows:]
            chosen = lax.shift_right_logical(where_to, 8) == lax.broadcasted_iota(jnp.int32, (elements, width), 0)
            picked = [
                jnp.sum(jnp.where(chosen, spread[p * elements : (p + 1) * elements], 0.0), axis=0, keepdims=True)
                for p in range(probes)
            ]
            faces[l] = jnp.concatenate(
                [picked[p][:, j * LANES : (j + 1) * LANES] for j in range(pieces) for p in range(probes)], axis=0
            )
            return carry

        lax.fori_loop(0, slots, one_slot, 0)

    def exchange(step, arriving):
        face_blocks = [faces[l] for l in range(slots)]

        def fill(d, carry):
            block = jnp.zeros((8, LANES), f32)
            for l in range(slots):
                block = jnp.where(link_of[l] == d, face_blocks[l], block)
            departing[step, d] = block
            return carry

        lax.fori_loop(0, nz, fill, 0)
        arriving[me] = jnp.zeros((8, LANES), f32)
        if step == 0:
            pl.semaphore_wait(barrier, nz - 1 + nxy - 1)

        def send(j, carry):
            peer = z_peer(j)
            pltpu.make_async_remote_copy(
                src_ref=departing.at[step, peer],
                dst_ref=arriving.at[me],
                send_sem=send_sems.at[step],
                recv_sem=recv_sems.at[step],
                device_id=(ix, iy, peer),
                device_id_type=MESH,
            ).start()
            return carry

        lax.fori_loop(0, nz - 1, send, 0)

    def land(buffer, sem, count):
        pltpu.make_async_copy(buffer.at[pl.ds(0, count)], buffer.at[pl.ds(0, count)], sem).wait()

    def scatter(step, arriving):
        land(arriving, recv_sems.at[step], nz - 1)

        def pick(s, blocks):
            block = arriving[s]
            return tuple(jnp.where(link_of[l] == s, block, blocks[l]) for l in range(slots))

        received = lax.fori_loop(0, nz, pick, tuple(jnp.zeros((8, LANES), f32) for _ in range(slots)))
        for l in range(slots):
            faces[l] = received[l]
        placed[...] = jnp.zeros_like(placed)

        def one_slot(l, carry):
            where_to = index[pl.ds(l, 1), :]
            chosen = lax.shift_right_logical(where_to, 8) == lax.broadcasted_iota(jnp.int32, (elements, width), 0)
            high = faces[l].astype(bf16).astype(f32)
            low = faces[l] - high
            spread = jnp.concatenate(
                [
                    jnp.where(
                        chosen,
                        jnp.concatenate([part[j * probes + p : j * probes + p + 1] for j in range(pieces)], axis=1),
                        0.0,
                    )
                    for part in (high, low)
                    for p in range(probes)
                ],
                axis=0,
            ).astype(bf16)
            placed[...] += nt_dot(spread, onehot[l])
            return carry

        lax.fori_loop(0, slots, one_slot, 0)
        return placed[:rows] + placed[rows:]

    loads[0].wait()
    first_pre = per_element(source, p_high, p_low) * inverse_rows
    gather(first_pre, True)
    exchange(0, arriving_a)
    loads[6].wait()
    k_high[...], k_low[...] = halves(k_raw[...])
    local_part = per_element(first_pre, k_high, k_low) * visc_rows
    first_img = (local_part - coupling * scatter(0, arriving_a)) * live_rows
    second_pre = per_element(first_img, p_high, p_low) * inverse_rows
    gather(second_pre, False)
    exchange(1, arriving_b)
    local_part = per_element(second_pre, k_high, k_low) * visc_rows
    second_img = (local_part - coupling * scatter(1, arriving_b)) * live_rows

    lane = lax.broadcasted_iota(jnp.int32, (1, LANES), 1)
    partial = jnp.zeros((1, LANES), f32)
    pairs = (
        (first_img, first_img), (first_img, second_img), (second_img, second_img),
        (first_img, source), (second_img, source),
    )
    for q, (a, b) in enumerate(pairs):
        product = a * b
        for p in range(probes):
            column = jnp.sum(product[p * elements : (p + 1) * elements], axis=0, keepdims=True)
            value = jnp.sum(column, axis=1, keepdims=True)
            partial = jnp.where(lane == q * probes + p, value, partial)

    def all_sum(buffer, mine, count, stage, device_of, part):
        buffer[mine] = part

        def send(j, carry):
            pltpu.make_async_remote_copy(
                src_ref=buffer.at[mine],
                dst_ref=buffer.at[mine],
                send_sem=send_sems.at[stage],
                recv_sem=recv_sems.at[stage],
                device_id=device_of(j),
                device_id_type=MESH,
            ).start()
            return carry

        lax.fori_loop(0, count - 1, send, 0)
        land(buffer, recv_sems.at[stage], count - 1)
        total = buffer[0]
        for s in range(1, count):
            total = total + buffer[s]
        return total

    def xy_device(j):
        other = xy_peer(j)
        return (other // ny, other % ny, me)

    total = all_sum(sums_z, me, nz, 2, lambda j: (ix, iy, z_peer(j)), partial)
    total = all_sum(sums_xy, plane, nxy, 3, xy_device, total)

    for p in range(probes):
        self_one, cross_mid, self_two, load_one, load_two = (
            jnp.sum(jnp.where(lane == q * probes + p, total, 0.0), axis=1, keepdims=True) for q in range(5)
        )
        determinant = self_one * self_two - cross_mid * cross_mid
        weight_one = (self_two * load_one - cross_mid * load_two) / determinant
        weight_two = (self_one * load_two - cross_mid * load_one) / determinant
        part = slice(p * elements, (p + 1) * elements)
        out_ref[part] = weight_one * first_pre[part] + weight_two * second_pre[part]

    land(departing.at[0], send_sems.at[0], nz - 1)
    land(departing.at[1], send_sems.at[1], nz - 1)
    land(sums_z, send_sems.at[2], nz - 1)
    land(sums_xy, send_sems.at[3], nxy - 1)


def solution(mesh):
    nx, ny, nz = (mesh.shape[name] for name in ("gx", "gy", "gz"))

    def per_device(rhs, viscosity, counts, neighbours, face_index, k_matrix, p_matrix):
        probes, elements, dofs = rhs.shape[3:]
        slots, width = face_index.shape[3:]
        rows = probes * elements
        vmem = pltpu.VMEM
        any_space = pl.BlockSpec(memory_space=pl.ANY)
        out = pl.pallas_call(
            functools.partial(kernel, nx, ny, nz, slots, probes, elements, dofs, width),
            out_shape=jax.ShapeDtypeStruct((rows, dofs), f32),
            in_specs=[any_space] * 7,
            out_specs=pl.BlockSpec(memory_space=vmem),
            scratch_shapes=[
                vmem((rows, dofs), f32),
                vmem((1, elements), f32),
                vmem((1, 1), jnp.int32),
                vmem((1, slots), jnp.int32),
                vmem((slots, width), jnp.int32),
                vmem((dofs, dofs), f32),
                vmem((dofs, dofs), f32),
                vmem((dofs, dofs), bf16),
                vmem((dofs, dofs), bf16),
                vmem((dofs, dofs), bf16),
                vmem((dofs, dofs), bf16),
                vmem((slots, dofs, width), bf16),
                vmem((slots, 8, LANES), f32),
                vmem((2, nz, 8, LANES), f32),
                vmem((nz, 8, LANES), f32),
                vmem((nz, 8, LANES), f32),
                vmem((2 * rows, dofs), f32),
                vmem((nz, 1, LANES), f32),
                vmem((nx * ny, 1, LANES), f32),
                pltpu.SemaphoreType.DMA((7,)),
                pltpu.SemaphoreType.DMA((4,)),
                pltpu.SemaphoreType.DMA((4,)),
            ],
            compiler_params=pltpu.CompilerParams(collective_id=0, has_side_effects=True),
        )(
            rhs.reshape(rows, dofs),
            viscosity.reshape(1, elements),
            counts.reshape(1, 1),
            neighbours.reshape(1, slots),
            face_index.reshape(slots, width),
            k_matrix,
            p_matrix,
        )
        return out.reshape(rhs.shape)

    return jax.shard_map(
        per_device,
        mesh=mesh,
        in_specs=(
            P("gx", "gy", "gz", None, None, None),
            P("gx", "gy", "gz", None),
            P("gx", "gy", "gz"),
            P("gx", "gy", "gz", None),
            P("gx", "gy", "gz", None, None),
            P(),
            P(),
        ),
        out_specs=P("gx", "gy", "gz", None, None, None),
        check_vma=False,
    )
```

time: 623 us -> 74.2 us (0.12)
  blocking collectives: 288 us -> 0 us
  other arithmetic: 109 us -> 0 us
  waiting for transfers between devices: 106 us -> 0 us
  local copies, waits for them, and re-layouts: 99.4 us -> 1.57 us
  Pallas kernels: 0 us -> 71.8 us
  between operations: 14.3 us -> 0.66 us
    psum x2 -> x0, blocking collectives: 243 us -> none  [the longest x1 122 us: per_device(): lax.psum((inner_prod(source, source), inner_prod(source, image_raw), inne...]
    all_gather x2 -> x0, waiting for transfers between devices: 106 us -> none  [shared_faces(): face_vals = lax.all_gather(flat_rows[None], 'gz', axis=0, tiled=True)]
    scatter-add x2 -> x0, other arithmetic: 96 us -> none  [operate(): jnp.zeros((probes, elements * dofs), jnp.float32).at[:, flat_index]]
    pallas_call x0 -> x1, Pallas kernels: none -> 71.8 us  [per_device(): pl.pallas_call(functools.partial(kernel, nx, ny, nz, slots, probes, eleme...]
    gather x2 -> x0, local copies, waits for them, and re-layouts: 62.2 us -> none  [operate(): flat_vec[:, flat_index].reshape(probes, slots, width).transpose(1, 0, 2)]
    all_gather x1 -> x0, blocking collectives: 44.4 us -> none  [shared_faces(): link_rows = lax.all_gather(links[None], 'gz', axis=0, tiled=True)]
    reshape x6 -> x0, local copies, waits for them, and re-layouts: 20.2 us -> none  [the longest x2 9.28 us: operate(): flat_vec = vector.reshape(probes, elements * dofs)]
    mul x3 -> x0, other arithmetic: 11.6 us -> none  [the longest x2 11.4 us: operate(): coupling * placed.reshape(vector.shape)]
  transfers between devices with their start and end apart: 2 -> 0, of which waited for: 2 -> 0; matrix products, arithmetic and copies ran while one was open for 0% -> 0% of each run, Pallas kernels for 0% -> 0%
where the time goes in v1:
time: 74.2 us; the launch traced here: 74 us
  Pallas kernels  71.8 us (97%)
  local copies, waits for them, and re-layouts  1.57 us (2%)
    pallas_call x1, Pallas kernels, per_device(): pl.pallas_call(functools.partial(kernel, nx, ny, nz, slots, probes, eleme...  71.8 us
    unnamed x1, local copies, waits for them, and re-layouts  1.57 us

profile of v1, /device:TPU:1, one launch (start us, length us, event | category | flops | bytes accessed | tf_op | source)
XLA Modules:
  0.0 74.0 jit_solution(13961748527608232061)
XLA Ops:
  0.7 71.8 %shard_map.73 = f32[128,256]{1,0:T(8,128)} custom-call(f32[128,256]{1,0:T(8,128)} %bitcast.8, f32[1,64]{1,0:T(1,128)} %bitcast.10, s32[1,1]{1,0:T(1,128)} %bitcast.6.counts_hbm, s32[1,16]{1,0:T(1,128)} %bitcast.11, s32[16,512]{1,0:T(8,128)} %bitcast.9, f32[256,256]{1,0:T(8,128)} %k_hbm.1, f32[256,256]{1,0:T(8,128)} %p_hbm.1), custom_call_target="tpu_custom_call" | custom-call | tf_op jit(solution)/shard_map/pallas_call | solution.py:276
  72.5 1.6 %copy.10 = f32[1,1,1,2,64,256]{5,4,3,2,1,0:T(8,128)} copy(f32[1,1,1,2,64,256]{5,4,3,2,1,0:T(8,128)} %bitcast.7) | data formatting | bytes 262144

commit v2 on v1

v2 whole, which is shorter than its diff:
```python
import functools

import jax
import jax.numpy as jnp
from jax import lax
from jax.experimental import pallas as pl
from jax.experimental.pallas import tpu as pltpu
from jax.sharding import PartitionSpec as P

MESH = pl.DeviceIdType.MESH
coupling = 0.5
LANES = 128
f32 = jnp.float32
bf16 = jnp.bfloat16


def halves(x):
    high = x.astype(bf16)
    low = (x - high.astype(f32)).astype(bf16)
    return high, low


def nn_dot(a, b):
    return lax.dot_general(a, b, (((1,), (0,)), ((), ())), preferred_element_type=f32)


def nt_dot(a, b):
    return lax.dot_general(a, b, (((1,), (1,)), ((), ())), preferred_element_type=f32)


def kernel(
    nx, ny, nz, slots, probes, elements, dofs, width,
    rhs_hbm, visc_hbm, counts_hbm, links_hbm, index_hbm, k_hbm, p_hbm,
    pre_one_out, pre_two_out, weights_ref,
    rhs, visc, counts, links, index, k_raw, p_raw,
    k_high, k_low, p_high, p_low, peer_index, onehot, onehot_t, faces, departing, arriving, placed,
    pre_one, pre_two, sums_z, sums_xy, load_sems, out_sems, send_sems, recv_sems, sum_sems,
):
    ix, iy, me = lax.axis_index("gx"), lax.axis_index("gy"), lax.axis_index("gz")
    chip, core = me // 2, me % 2
    chips = nz // 2
    half = chips // 2
    nxy = nx * ny
    plane = ix * ny + iy
    rows = probes * elements
    pieces = width // LANES
    span = 4 * width
    shift = dofs.bit_length() - 1

    def z_peer(j):
        offset = nz // 2 + ((j + 1) // 2) * (1 - 2 * (j % 2))
        return lax.rem(me + offset, nz)

    def xy_peer(j):
        return lax.rem(plane + 1 + j, nxy)

    def group_chip(group, side):
        away = group + 1
        offset = away if side == 0 else -away * (1 - away // half)
        return lax.rem(chip + offset + chips, chips)

    barrier = pltpu.get_barrier_semaphore()

    def greet_z(j, carry):
        pl.semaphore_signal(barrier, inc=1, device_id=(ix, iy, z_peer(j)), device_id_type=MESH)
        return carry

    def greet_xy(j, carry):
        other = xy_peer(j)
        pl.semaphore_signal(barrier, inc=1, device_id=(other // ny, other % ny, me), device_id_type=MESH)
        return carry

    loads = [
        pltpu.make_async_copy(src, dst, load_sems.at[i])
        for i, (src, dst) in enumerate(
            (
                (index_hbm, index), (rhs_hbm, rhs), (p_hbm, p_raw), (visc_hbm, visc),
                (counts_hbm, counts), (links_hbm, links), (k_hbm, k_raw),
            )
        )
    ]
    for load in loads:
        load.start()
    lax.fori_loop(0, nz - 1, greet_z, 0)
    lax.fori_loop(0, nxy - 1, greet_xy, 0)

    loads[3].wait()
    loads[4].wait()
    loads[5].wait()
    element_id = lax.broadcasted_iota(jnp.int32, (elements, 1), 0)
    live = (element_id < counts[0:1, 0:1]).astype(f32)
    diagonal = lax.broadcasted_iota(jnp.int32, (elements, elements), 0) == lax.broadcasted_iota(
        jnp.int32, (elements, elements), 1
    )
    visc_col = jnp.sum(jnp.where(diagonal, visc[0:1, :], 0.0), axis=1, keepdims=True)
    live_rows = jnp.concatenate([live] * probes, axis=0)
    visc_rows = jnp.concatenate([visc_col] * probes, axis=0)
    inverse_rows = live_rows / visc_rows

    loads[1].wait()
    loads[2].wait()
    p_high[...], p_low[...] = halves(p_raw[...])
    source = jnp.where(live_rows > 0.0, rhs[...], 0.0)

    def per_element(x, m_high, m_low):
        high, low = halves(x)
        both = nn_dot(jnp.concatenate([high, low], axis=0), m_high[...])
        return both[:rows] + both[rows:] + nn_dot(high, m_low[...])

    link_of = [jnp.broadcast_to(links[0:1, l : l + 1], (8, LANES)) for l in range(slots)]

    def hot_of(row):
        ids = lax.broadcasted_iota(jnp.int32, (dofs, row.shape[1]), 0)
        return jnp.where((row & (dofs - 1)) == ids, 1.0, 0.0).astype(bf16)

    def chosen_of(row):
        return lax.shift_right_arithmetic(row, shift) == lax.broadcasted_iota(jnp.int32, (elements, row.shape[1]), 0)

    def pick_faces(stacked, hot, row):
        spread = nn_dot(stacked, hot)
        spread = spread[:rows] + spread[rows:]
        chosen = chosen_of(row)
        picked = [
            jnp.sum(jnp.where(chosen, spread[p * elements : (p + 1) * elements], 0.0), axis=0, keepdims=True)
            for p in range(probes)
        ]
        return jnp.concatenate(
            [picked[p][:, j * LANES : (j + 1) * LANES] for j in range(pieces) for p in range(probes)], axis=0
        )

    def gather_slots(x):
        stacked = jnp.concatenate(halves(x), axis=0)

        def one_slot(l, carry):
            row = index[pl.ds(l, 1), :]
            faces[l] = pick_faces(stacked, hot_of(row), row)
            return carry

        lax.fori_loop(0, slots, one_slot, 0)

    def fill_departing():
        face_blocks = [faces[l] for l in range(slots)]

        def fill_group(group, carry):
            for side in range(2):
                for other in range(2):
                    peer = group_chip(group, side) * 2 + other
                    block = jnp.zeros((8, LANES), f32)
                    for l in range(slots):
                        block = jnp.where(link_of[l] == peer, face_blocks[l], block)
                    departing[0, group * 4 + side * 2 + other] = block
            return carry

        lax.fori_loop(0, half, fill_group, 0)

    def send_one(step, group, side, other, landing_side):
        pltpu.make_async_remote_copy(
            src_ref=departing.at[step, group * 4 + side * 2 + other],
            dst_ref=arriving.at[step, group * 4 + landing_side * 2 + core],
            send_sem=send_sems.at[step],
            recv_sem=recv_sems.at[step, group],
            device_id=(ix, iy, group_chip(group, side) * 2 + other),
            device_id_type=MESH,
        ).start()

    def send_last(step):
        send_one(step, half - 1, 0, 0, 0)
        send_one(step, half - 1, 0, 1, 0)
        send_one(step, half - 1, 1, 1 - core, 1)

    def send_group(step, group):
        for side in range(2):
            for other in range(2):
                send_one(step, group, side, other, 1 - side)

    def group_row(group):
        return jnp.concatenate([peer_index[pl.ds(group * 4 + r, 1), :] for r in range(4)], axis=1)

    def make_peer_index():
        peer_number = lax.broadcasted_iota(jnp.int32, (nz, width), 0)
        away = peer_number // 4 + 1
        offset = jnp.where((peer_number // 2) % 2 == 0, away, jnp.where(away == half, 0, -away))
        place = chip + offset
        place = jnp.where(place < 0, place + chips, jnp.where(place >= chips, place - chips, place))
        peer = place * 2 + peer_number % 2
        table = jnp.full((nz, width), -1, jnp.int32)
        for l in range(slots):
            table = jnp.where(links[0:1, l : l + 1] == peer, index[l : l + 1, :], table)
        peer_index[...] = table

    def make_onehots(group, carry):
        for r in range(4):
            hot = hot_of(peer_index[pl.ds(group * 4 + r, 1), :])
            onehot[group, :, r * width : (r + 1) * width] = hot
            onehot_t[group, r * width : (r + 1) * width, :] = hot.T
        return carry

    def gather_and_send(x):
        stacked = jnp.concatenate(halves(x), axis=0)

        def gather_group(group):
            for r in range(4):
                departing[1, group * 4 + r] = pick_faces(
                    stacked, onehot[group, :, r * width : (r + 1) * width], peer_index[pl.ds(group * 4 + r, 1), :]
                )

        gather_group(half - 1)
        send_last(1)

        def body(t, carry):
            group = half - 2 - t
            gather_group(group)
            send_group(1, group)
            return carry

        lax.fori_loop(0, half - 1, body, 0)

    def land(buffer, sem, count):
        pltpu.make_async_copy(buffer.at[pl.ds(0, count)], buffer.at[pl.ds(0, count)], sem).wait()

    def add_group(step, group, count):
        land(arriving.at[step], recv_sems.at[step, group], count)
        chosen = chosen_of(group_row(group))
        blocks = [arriving[step, group * 4 + r] for r in range(4)]
        highs = [block.astype(bf16).astype(f32) for block in blocks]
        lows = [block - high for block, high in zip(blocks, highs)]
        spread = jnp.concatenate(
            [
                jnp.where(
                    chosen,
                    jnp.concatenate(
                        [part[j * probes + p : j * probes + p + 1] for part in parts for j in range(pieces)], axis=1
                    ),
                    0.0,
                )
                for parts in (highs, lows)
                for p in range(probes)
            ],
            axis=0,
        ).astype(bf16)
        placed[...] += nn_dot(spread, onehot_t[group])

    def receive(step):
        placed[...] = jnp.zeros_like(placed)

        def body(group, carry):
            add_group(step, group, 4)
            return carry

        lax.fori_loop(0, half - 1, body, 0)
        add_group(step, half - 1, 3)
        return placed[:rows] + placed[rows:]

    for step in range(2):
        arriving[step, (half - 1) * 4 + 2 + core] = jnp.zeros((8, LANES), f32)
    first_pre = per_element(source, p_high, p_low) * inverse_rows
    pre_one[...] = first_pre
    pltpu.make_async_copy(pre_one, pre_one_out, out_sems.at[0]).start()
    loads[0].wait()
    gather_slots(first_pre)
    fill_departing()
    pl.semaphore_wait(barrier, nz - 1 + nxy - 1)
    send_last(0)

    def send_body(t, carry):
        send_group(0, half - 2 - t)
        return carry

    lax.fori_loop(0, half - 1, send_body, 0)
    make_peer_index()
    lax.fori_loop(0, half, make_onehots, 0)
    loads[6].wait()
    k_high[...], k_low[...] = halves(k_raw[...])
    local_part = per_element(first_pre, k_high, k_low) * visc_rows
    first_img = (local_part - coupling * receive(0)) * live_rows
    second_pre = per_element(first_img, p_high, p_low) * inverse_rows
    gather_and_send(second_pre)
    pre_two[...] = second_pre
    pltpu.make_async_copy(pre_two, pre_two_out, out_sems.at[1]).start()

    lane = lax.broadcasted_iota(jnp.int32, (1, LANES), 1)

    def note(partial, q, a, b):
        product = a * b
        for p in range(probes):
            column = jnp.sum(product[p * elements : (p + 1) * elements], axis=0, keepdims=True)
            value = jnp.sum(column, axis=1, keepdims=True)
            partial = jnp.where(lane == q * probes + p, value, partial)
        return partial

    partial = jnp.zeros((1, LANES), f32)
    partial = note(partial, 0, first_img, first_img)
    partial = note(partial, 3, first_img, source)
    local_part = per_element(second_pre, k_high, k_low) * visc_rows
    second_img = (local_part - coupling * receive(1)) * live_rows
    partial = note(partial, 1, first_img, second_img)
    partial = note(partial, 2, second_img, second_img)
    partial = note(partial, 4, second_img, source)

    def all_sum(buffer, mine, count, stage, device_of, part):
        buffer[mine] = part

        def send(j, carry):
            pltpu.make_async_remote_copy(
                src_ref=buffer.at[mine],
                dst_ref=buffer.at[mine],
                send_sem=send_sems.at[2 + stage],
                recv_sem=sum_sems.at[stage],
                device_id=device_of(j),
                device_id_type=MESH,
            ).start()
            return carry

        lax.fori_loop(0, count - 1, send, 0)
        land(buffer, sum_sems.at[stage], count - 1)
        total = buffer[0]
        for s in range(1, count):
            total = total + buffer[s]
        return total

    def xy_device(j):
        other = xy_peer(j)
        return (other // ny, other % ny, me)

    total = all_sum(sums_z, me, nz, 0, lambda j: (ix, iy, z_peer(j)), partial)
    total = all_sum(sums_xy, plane, nxy, 1, xy_device, total)

    for p in range(probes):
        self_one, cross_mid, self_two, load_one, load_two = (
            jnp.sum(jnp.where(lane == q * probes + p, total, 0.0), axis=1, keepdims=True) for q in range(5)
        )
        determinant = self_one * self_two - cross_mid * cross_mid
        weight_one = (self_two * load_one - cross_mid * load_two) / determinant
        weight_two = (self_one * load_two - cross_mid * load_one) / determinant
        weights_ref[p : p + 1] = jnp.broadcast_to(weight_one, (1, LANES))
        weights_ref[probes + p : probes + p + 1] = jnp.broadcast_to(weight_two, (1, LANES))

    pltpu.make_async_copy(pre_one, pre_one_out, out_sems.at[0]).wait()
    pltpu.make_async_copy(pre_two, pre_two_out, out_sems.at[1]).wait()
    land(departing.at[0], send_sems.at[0], nz - 1)
    land(departing.at[1], send_sems.at[1], nz - 1)
    land(sums_z, send_sems.at[2], nz - 1)
    land(sums_xy, send_sems.at[3], nxy - 1)


def solution(mesh):
    nx, ny, nz = (mesh.shape[name] for name in ("gx", "gy", "gz"))

    def per_device(rhs, viscosity, counts, neighbours, face_index, k_matrix, p_matrix):
        probes, elements, dofs = rhs.shape[3:]
        slots, width = face_index.shape[3:]
        rows = probes * elements
        vmem = pltpu.VMEM
        any_space = pl.BlockSpec(memory_space=pl.ANY)
        field = jax.ShapeDtypeStruct((rows, dofs), f32)
        half = nz // 4
        first_pre, second_pre, weights = pl.pallas_call(
            functools.partial(kernel, nx, ny, nz, slots, probes, elements, dofs, width),
            out_shape=(field, field, jax.ShapeDtypeStruct((2 * probes, LANES), f32)),
            in_specs=[any_space] * 7,
            out_specs=(any_space, any_space, pl.BlockSpec(memory_space=vmem)),
            scratch_shapes=[
                vmem((rows, dofs), f32),
                vmem((1, elements), f32),
                vmem((1, 1), jnp.int32),
                vmem((1, slots), jnp.int32),
                vmem((slots, width), jnp.int32),
                vmem((dofs, dofs), f32),
                vmem((dofs, dofs), f32),
                vmem((dofs, dofs), bf16),
                vmem((dofs, dofs), bf16),
                vmem((dofs, dofs), bf16),
                vmem((dofs, dofs), bf16),
                vmem((nz, width), jnp.int32),
                vmem((half, dofs, 4 * width), bf16),
                vmem((half, 4 * width, dofs), bf16),
                vmem((slots, 8, LANES), f32),
                vmem((2, nz, 8, LANES), f32),
                vmem((2, nz, 8, LANES), f32),
                vmem((2 * rows, dofs), f32),
                vmem((rows, dofs), f32),
                vmem((rows, dofs), f32),
                vmem((nz, 1, LANES), f32),
                vmem((nx * ny, 1, LANES), f32),
                pltpu.SemaphoreType.DMA((7,)),
                pltpu.SemaphoreType.DMA((2,)),
                pltpu.SemaphoreType.DMA((4,)),
                pltpu.SemaphoreType.DMA((2, half)),
                pltpu.SemaphoreType.DMA((2,)),
            ],
            compiler_params=pltpu.CompilerParams(collective_id=0, has_side_effects=True),
        )(
            rhs.reshape(rows, dofs),
            viscosity.reshape(1, elements),
            counts.reshape(1, 1),
            neighbours.reshape(1, slots),
            face_index.reshape(slots, width),
            k_matrix,
            p_matrix,
        )
        scale_one = weights[:probes, 0][:, None, None]
        scale_two = weights[probes:, 0][:, None, None]
        shape = (probes, elements, dofs)
        out = scale_one * first_pre.reshape(shape) + scale_two * second_pre.reshape(shape)
        return out.reshape(rhs.shape)

    return jax.shard_map(
        per_device,
        mesh=mesh,
        in_specs=(
            P("gx", "gy", "gz", None, None, None),
            P("gx", "gy", "gz", None),
            P("gx", "gy", "gz"),
            P("gx", "gy", "gz", None),
            P("gx", "gy", "gz", None, None),
            P(),
            P(),
        ),
        out_specs=P("gx", "gy", "gz", None, None, None),
        check_vma=False,
    )
```

time: 74.2 us -> 66.7 us (0.90)
  Pallas kernels: 71.8 us -> 63.3 us
  other arithmetic: 0 us -> 1.72 us
  local copies, waits for them, and re-layouts: 1.57 us -> 0.8 us
    pallas_call x1, Pallas kernels: 71.8 us -> 63.3 us  [per_device(): pl.pallas_call(functools.partial(kernel, nx, ny, nz, slots, probes, eleme...]
    add x0 -> x1, other arithmetic: none -> 1.72 us  [per_device(): scale_one * first_pre.reshape(shape) + scale_two * second_pre.reshape(shape)]
    unnamed x1 -> x2, local copies, waits for them, and re-layouts: 1.57 us -> 0.66 us
where the time goes in v2:
time: 66.7 us; the launch traced here: 66.5 us
  Pallas kernels  63.3 us (95%)
  other arithmetic  1.72 us (3%)
  local copies, waits for them, and re-layouts  0.8 us (1%)
  between operations  0.67 us (1%)
    pallas_call x1, Pallas kernels, per_device(): pl.pallas_call(functools.partial(kernel, nx, ny, nz, slots, probes, eleme...  63.3 us
    add x1, other arithmetic, per_device(): scale_one * first_pre.reshape(shape) + scale_two * second_pre.reshape(shape)  1.72 us

profile of v2, /device:TPU:1, one launch (start us, length us, event | category | flops | bytes accessed | tf_op | source)
XLA Modules:
  0.0 66.5 jit_solution(10669397461664149197)
XLA Ops:
  0.7 63.3 %shard_map.73 = (f32[128,256]{1,0:T(8,128)}, f32[128,256]{1,0:T(8,128)}, f32[4,128]{1,0:T(4,128)}) custom-call(f32[128,256]{1,0:T(8,128)} %bitcast.10, f32[1,64]{1,0:T(1,128)} %bitcast.12, s32[1,1]{1,0:T(1,128)} %bitcast.7.counts_hbm, s32[1,16]{1,0:T(1,128)} %bitcast.13, s32[16,512]{1,0:T(8,128)} %bitcast.11, f32[256,256]{1,0:T(8,128)} %k_hbm.1, ...), custom_call_target="tpu_custom_call" | custom-call | tf_op jit(solution)/shard_map/pallas_call | solution.py:357
  64.0 0.0 copy-start
  64.0 0.7 copy-done
  64.6 0.1 slice_reduce_fusion.1
  64.8 1.7 %multiply_add_fusion = f32[1,1,1,2,64,256]{5,4,3,2,1,0:T(8,128)} fusion(f32[1,1,1,2,64,256]{5,4,3,2,1,0:T(8,128)} %bitcast.9, f32[1,1,1,2,64,256]{5,4,3,2,1,0:T(8,128)} %bitcast.8, f32[2]{0:T(128)S(1)} %get-tuple-element.12, f32[2]{0:T(128)S(1)} %get-tuple-element.11), kind=kLoop, calls=%fused_computation | loop fusion | flops 98304 | bytes 393232 | tf_op jit(solution)/shard_map/add | solution.py:404
Async XLA Ops:
  64.0 0.7 %copy-start = (f32[4,128]{1,0:T(4,128)S(1)}, f32[4,128]{1,0:T(4,128)}, u32[]{:S(2)}) copy-start(f32[4,128]{1,0:T(4,128)} %get-tuple-element.8) | copy-start | bytes 6148

commit v3 on v2

--- a/solution.py
+++ b/solution.py
@@ -31,10 +31,10 @@
 def kernel(
     nx, ny, nz, slots, probes, elements, dofs, width,
     rhs_hbm, visc_hbm, counts_hbm, links_hbm, index_hbm, k_hbm, p_hbm,
-    pre_one_out, pre_two_out, weights_ref,
+    out_ref,
     rhs, visc, counts, links, index, k_raw, p_raw,
     k_high, k_low, p_high, p_low, peer_index, onehot, onehot_t, faces, departing, arriving, placed,
-    pre_one, pre_two, sums_z, sums_xy, load_sems, out_sems, send_sems, recv_sems, sum_sems,
+    sums_z, sums_xy, load_sems, send_sems, recv_sems, sum_sems,
 ):
     ix, iy, me = lax.axis_index("gx"), lax.axis_index("gy"), lax.axis_index("gz")
     chip, core = me // 2, me % 2
@@ -44,7 +44,6 @@
     plane = ix * ny + iy
     rows = probes * elements
     pieces = width // LANES
-    span = 4 * width
     shift = dofs.bit_length() - 1
 
     def z_peer(j):
@@ -153,28 +152,26 @@
 
         lax.fori_loop(0, half, fill_group, 0)
 
-    def send_one(step, group, side, other, landing_side):
+    def send_one(step, group, side, other, landing_side, box=None):
         pltpu.make_async_remote_copy(
             src_ref=departing.at[step, group * 4 + side * 2 + other],
             dst_ref=arriving.at[step, group * 4 + landing_side * 2 + core],
             send_sem=send_sems.at[step],
-            recv_sem=recv_sems.at[step, group],
+            recv_sem=recv_sems.at[step, group if box is None else box],
             device_id=(ix, iy, group_chip(group, side) * 2 + other),
             device_id_type=MESH,
         ).start()
 
-    def send_last(step):
-        send_one(step, half - 1, 0, 0, 0)
-        send_one(step, half - 1, 0, 1, 0)
-        send_one(step, half - 1, 1, 1 - core, 1)
+    def send_far(step, other):
+        send_one(step, half - 1, 0, other, 0)
+
+    def send_twin(step):
+        send_one(step, half - 1, 1, 1 - core, 1, half)
 
     def send_group(step, group):
         for side in range(2):
             for other in range(2):
                 send_one(step, group, side, other, 1 - side)
-
-    def group_row(group):
-        return jnp.concatenate([peer_index[pl.ds(group * 4 + r, 1), :] for r in range(4)], axis=1)
 
     def make_peer_index():
         peer_number = lax.broadcasted_iota(jnp.int32, (nz, width), 0)
@@ -198,30 +195,35 @@
     def gather_and_send(x):
         stacked = jnp.concatenate(halves(x), axis=0)
 
-        def gather_group(group):
-            for r in range(4):
-                departing[1, group * 4 + r] = pick_faces(
-                    stacked, onehot[group, :, r * width : (r + 1) * width], peer_index[pl.ds(group * 4 + r, 1), :]
-                )
-
-        gather_group(half - 1)
-        send_last(1)
+        def gather_one(slot, group, r):
+            departing[1, slot] = pick_faces(
+                stacked, onehot[group, :, r * width : (r + 1) * width], peer_index[pl.ds(slot, 1), :]
+            )
+
+        for other in range(2):
+            gather_one((half - 1) * 4 + other, half - 1, other)
+            send_far(1, other)
 
         def body(t, carry):
             group = half - 2 - t
-            gather_group(group)
+            for side in range(2):
+                for other in range(2):
+                    gather_one(group * 4 + side * 2 + other, group, side * 2 + other)
             send_group(1, group)
             return carry
 
         lax.fori_loop(0, half - 1, body, 0)
+        for other in range(2):
+            gather_one((half - 1) * 4 + 2 + other, half - 1, 2 + other)
+        send_twin(1)
 
     def land(buffer, sem, count):
         pltpu.make_async_copy(buffer.at[pl.ds(0, count)], buffer.at[pl.ds(0, count)], sem).wait()
 
-    def add_group(step, group, count):
-        land(arriving.at[step], recv_sems.at[step, group], count)
-        chosen = chosen_of(group_row(group))
-        blocks = [arriving[step, group * 4 + r] for r in range(4)]
+    def addend(step, group, first, count):
+        row = jnp.concatenate([peer_index[pl.ds(group * 4 + r, 1), :] for r in range(first, first + count)], axis=1)
+        chosen = chosen_of(row)
+        blocks = [arriving[step, group * 4 + r] for r in range(first, first + count)]
         highs = [block.astype(bf16).astype(f32) for block in blocks]
         lows = [block - high for block, high in zip(blocks, highs)]
         spread = jnp.concatenate(
@@ -238,35 +240,38 @@
             ],
             axis=0,
         ).astype(bf16)
-        placed[...] += nn_dot(spread, onehot_t[group])
+        return nn_dot(spread, onehot_t[group, first * width : (first + count) * width, :])
 
     def receive(step):
-        placed[...] = jnp.zeros_like(placed)
+        land(arriving.at[step], recv_sems.at[step, half], 1)
+        placed[...] = addend(step, half - 1, 2, 2)
 
         def body(group, carry):
-            add_group(step, group, 4)
+            land(arriving.at[step], recv_sems.at[step, group], 4)
+            placed[...] += addend(step, group, 0, 4)
             return carry
 
         lax.fori_loop(0, half - 1, body, 0)
-        add_group(step, half - 1, 3)
-        return placed[:rows] + placed[rows:]
+        land(arriving.at[step], recv_sems.at[step, half - 1], 2)
+        total = placed[...] + addend(step, half - 1, 0, 2)
+        return total[:rows] + total[rows:]
 
     for step in range(2):
         arriving[step, (half - 1) * 4 + 2 + core] = jnp.zeros((8, LANES), f32)
     first_pre = per_element(source, p_high, p_low) * inverse_rows
-    pre_one[...] = first_pre
-    pltpu.make_async_copy(pre_one, pre_one_out, out_sems.at[0]).start()
     loads[0].wait()
     gather_slots(first_pre)
     fill_departing()
     pl.semaphore_wait(barrier, nz - 1 + nxy - 1)
-    send_last(0)
+    send_far(0, 0)
+    send_far(0, 1)
 
     def send_body(t, carry):
         send_group(0, half - 2 - t)
         return carry
 
     lax.fori_loop(0, half - 1, send_body, 0)
+    send_twin(0)
     make_peer_index()
     lax.fori_loop(0, half, make_onehots, 0)
     loads[6].wait()
@@ -275,8 +280,6 @@
     first_img = (local_part - coupling * receive(0)) * live_rows
     second_pre = per_element(first_img, p_high, p_low) * inverse_rows
     gather_and_send(second_pre)
-    pre_two[...] = second_pre
-    pltpu.make_async_copy(pre_two, pre_two_out, out_sems.at[1]).start()
 
     lane = lax.broadcasted_iota(jnp.int32, (1, LANES), 1)
 
@@ -332,11 +335,9 @@
         determinant = self_one * self_two - cross_mid * cross_mid
         weight_one = (self_two * load_one - cross_mid * load_two) / determinant
         weight_two = (self_one * load_two - cross_mid * load_one) / determinant
-        weights_ref[p : p + 1] = jnp.broadcast_to(weight_one, (1, LANES))
-        weights_ref[probes + p : probes + p + 1] = jnp.broadcast_to(weight_two, (1, LANES))
-
-    pltpu.make_async_copy(pre_one, pre_one_out, out_sems.at[0]).wait()
-    pltpu.make_async_copy(pre_two, pre_two_out, out_sems.at[1]).wait()
+        part = slice(p * elements, (p + 1) * elements)
+        out_ref[part] = weight_one * first_pre[part] + weight_two * second_pre[part]
+
     land(departing.at[0], send_sems.at[0], nz - 1)
     land(departing.at[1], send_sems.at[1], nz - 1)
     land(sums_z, send_sems.at[2], nz - 1)
@@ -351,14 +352,14 @@
         slots, width = face_index.shape[3:]
         rows = probes * elements
         vmem = pltpu.VMEM
-        any_space = pl.BlockSpec(memory_space=pl.ANY)
-        field = jax.ShapeDtypeStruct((rows, dofs), f32)
+        stay = functools.partial(pltpu.with_memory_space_constraint, memory_space=pltpu.HBM)
+        hbm = pl.BlockSpec(memory_space=pltpu.HBM)
         half = nz // 4
-        first_pre, second_pre, weights = pl.pallas_call(
+        out = pl.pallas_call(
             functools.partial(kernel, nx, ny, nz, slots, probes, elements, dofs, width),
-            out_shape=(field, field, jax.ShapeDtypeStruct((2 * probes, LANES), f32)),
-            in_specs=[any_space] * 7,
-            out_specs=(any_space, any_space, pl.BlockSpec(memory_space=vmem)),
+            out_shape=jax.ShapeDtypeStruct((rows, dofs), f32),
+            in_specs=[hbm] * 7,
+            out_specs=pl.BlockSpec(memory_space=vmem),
             scratch_shapes=[
                 vmem((rows, dofs), f32),
                 vmem((1, elements), f32),
@@ -378,30 +379,23 @@
                 vmem((2, nz, 8, LANES), f32),
                 vmem((2, nz, 8, LANES), f32),
                 vmem((2 * rows, dofs), f32),
-                vmem((rows, dofs), f32),
-                vmem((rows, dofs), f32),
                 vmem((nz, 1, LANES), f32),
                 vmem((nx * ny, 1, LANES), f32),
                 pltpu.SemaphoreType.DMA((7,)),
-                pltpu.SemaphoreType.DMA((2,)),
                 pltpu.SemaphoreType.DMA((4,)),
-                pltpu.SemaphoreType.DMA((2, half)),
+                pltpu.SemaphoreType.DMA((2, half + 1)),
                 pltpu.SemaphoreType.DMA((2,)),
             ],
-            compiler_params=pltpu.CompilerParams(collective_id=0, has_side_effects=True),
+            compiler_params=pltpu.CompilerParams(collective_id=0, has_side_effects=True, vmem_limit_bytes=24 * 1024 * 1024),
         )(
-            rhs.reshape(rows, dofs),
-            viscosity.reshape(1, elements),
+            stay(rhs.reshape(rows, dofs)),
+            stay(viscosity.reshape(1, elements)),
             counts.reshape(1, 1),
-            neighbours.reshape(1, slots),
-            face_index.reshape(slots, width),
-            k_matrix,
-            p_matrix,
+            stay(neighbours.reshape(1, slots)),
+            stay(face_index.reshape(slots, width)),
+            stay(k_matrix),
+            stay(p_matrix),
         )
-        scale_one = weights[:probes, 0][:, None, None]
-        scale_two = weights[probes:, 0][:, None, None]
-        shape = (probes, elements, dofs)
-        out = scale_one * first_pre.reshape(shape) + scale_two * second_pre.reshape(shape)
         return out.reshape(rhs.shape)
 
     return jax.shard_map(

time: 66.7 us -> 63.6 us (0.954)
  other arithmetic: 1.72 us -> 0 us
  Pallas kernels: 63.3 us -> 62.2 us
    add x1 -> x0, other arithmetic: 1.72 us -> none  [per_device(): scale_one * first_pre.reshape(shape) + scale_two * second_pre.reshape(shape)]
    pallas_call x1, Pallas kernels: 63.3 us -> 62.2 us  [per_device(): pl.pallas_call(functools.partial(kernel, nx, ny, nz, slots, probes, eleme...]
where the time goes in v3:
time: 63.6 us; the launch traced here: 63.5 us
  Pallas kernels  62.2 us (98%)
  local copies, waits for them, and re-layouts  0.66 us (1%)
  between operations  0.66 us (1%)
    pallas_call x1, Pallas kernels, per_device(): pl.pallas_call(functools.partial(kernel, nx, ny, nz, slots, probes, eleme...  62.2 us

profile of v3, /device:TPU:1, one launch (start us, length us, event | category | flops | bytes accessed | tf_op | source)
XLA Modules:
  0.0 63.5 jit_solution(84651859743704498)
XLA Ops:
  0.7 62.2 %shard_map.73 = f32[128,256]{1,0:T(8,128)S(1)} custom-call(f32[128,256]{1,0:T(8,128)} %bitcast.8, f32[1,64]{1,0:T(1,128)} %bitcast.10, s32[1,1]{1,0:T(1,128)} %bitcast.6.counts_hbm, s32[1,16]{1,0:T(1,128)} %bitcast.11, s32[16,512]{1,0:T(8,128)} %bitcast.9, f32[256,256]{1,0:T(8,128)} %k_hbm.1, f32[256,256]{1,0:T(8,128)} %p_hbm.1), custom_call_target="tpu_custom_call" | custom-call | tf_op jit(solution)/shard_map/pallas_call | solution.py:358
  62.8 0.7 %copy.10 = f32[1,1,1,2,64,256]{5,4,3,2,1,0:T(8,128)} copy(f32[1,1,1,2,64,256]{5,4,3,2,1,0:T(8,128)S(1)} %bitcast.7) | data formatting | bytes 262144

commit v4 on v3

--- a/solution.py
+++ b/solution.py
@@ -51,7 +51,9 @@
         return lax.rem(me + offset, nz)
 
     def xy_peer(j):
-        return lax.rem(plane + 1 + j, nxy)
+        across = nx // 2 + ((j // ny + 1) // 2) * (1 - 2 * ((j // ny) % 2))
+        along = ny // 2 + ((j % ny + 1) // 2) * (1 - 2 * ((j % ny) % 2))
+        return lax.rem(ix + across, nx) * ny + lax.rem(iy + along, ny)
 
     def group_chip(group, side):
         away = group + 1

time: 63.6 us -> 63.3 us (level)
  no operation moved by 1% of the time
where the time goes in v4:
time: 63.3 us; the launch traced here: 63.1 us
  Pallas kernels  61.8 us (98%)
  local copies, waits for them, and re-layouts  0.66 us (1%)
  between operations  0.66 us (1%)
    pallas_call x1, Pallas kernels, per_device(): pl.pallas_call(functools.partial(kernel, nx, ny, nz, slots, probes, eleme...  61.8 us

profile of v4, /device:TPU:1, one launch (start us, length us, event | category | flops | bytes accessed | tf_op | source)
XLA Modules:
  0.0 63.1 jit_solution(14636431314080599354)
XLA Ops:
  0.7 61.8 %shard_map.73 = f32[128,256]{1,0:T(8,128)S(1)} custom-call(f32[128,256]{1,0:T(8,128)} %bitcast.8, f32[1,64]{1,0:T(1,128)} %bitcast.10, s32[1,1]{1,0:T(1,128)} %bitcast.6.counts_hbm, s32[1,16]{1,0:T(1,128)} %bitcast.11, s32[16,512]{1,0:T(8,128)} %bitcast.9, f32[256,256]{1,0:T(8,128)} %k_hbm.1, f32[256,256]{1,0:T(8,128)} %p_hbm.1), custom_call_target="tpu_custom_call" | custom-call | tf_op jit(solution)/shard_map/pallas_call | solution.py:360
  62.5 0.7 %copy.10 = f32[1,1,1,2,64,256]{5,4,3,2,1,0:T(8,128)} copy(f32[1,1,1,2,64,256]{5,4,3,2,1,0:T(8,128)S(1)} %bitcast.7) | data formatting | bytes 262144

commit v5 on v4

--- a/solution.py
+++ b/solution.py
@@ -302,7 +302,7 @@
     partial = note(partial, 2, second_img, second_img)
     partial = note(partial, 4, second_img, source)
 
-    def all_sum(buffer, mine, count, stage, device_of, part):
+    def all_sum(buffer, mine, count, stage, device_of, part, left):
         buffer[mine] = part
 
         def send(j, carry):
@@ -317,6 +317,8 @@
             return carry
 
         lax.fori_loop(0, count - 1, send, 0)
+        for gone, sem in left:
+            land(gone, send_sems.at[sem], nz - 1)
         land(buffer, sum_sems.at[stage], count - 1)
         total = buffer[0]
         for s in range(1, count):
@@ -327,8 +329,8 @@
         other = xy_peer(j)
         return (other // ny, other % ny, me)
 
-    total = all_sum(sums_z, me, nz, 0, lambda j: (ix, iy, z_peer(j)), partial)
-    total = all_sum(sums_xy, plane, nxy, 1, xy_device, total)
+    total = all_sum(sums_z, me, nz, 0, lambda j: (ix, iy, z_peer(j)), partial, ((departing.at[0], 0), (departing.at[1], 1)))
+    total = all_sum(sums_xy, plane, nxy, 1, xy_device, total, ((sums_z, 2),))
 
     for p in range(probes):
         self_one, cross_mid, self_two, load_one, load_two = (
@@ -340,9 +342,6 @@
         part = slice(p * elements, (p + 1) * elements)
         out_ref[part] = weight_one * first_pre[part] + weight_two * second_pre[part]
 
-    land(departing.at[0], send_sems.at[0], nz - 1)
-    land(departing.at[1], send_sems.at[1], nz - 1)
-    land(sums_z, send_sems.at[2], nz - 1)
     land(sums_xy, send_sems.at[3], nxy - 1)
 
 

time: 63.3 us -> 63.3 us (level)
  no operation moved by 1% of the time
where the time goes in v5:
time: 63.3 us; the launch traced here: 63.1 us
  Pallas kernels  61.8 us (98%)
  local copies, waits for them, and re-layouts  0.66 us (1%)
  between operations  0.66 us (1%)
    pallas_call x1, Pallas kernels, per_device(): pl.pallas_call(functools.partial(kernel, nx, ny, nz, slots, probes, eleme...  61.8 us

profile of v5, /device:TPU:1, one launch (start us, length us, event | category | flops | bytes accessed | tf_op | source)
XLA Modules:
  0.0 63.1 jit_solution(13055101991565115063)
XLA Ops:
  0.7 61.8 %shard_map.73 = f32[128,256]{1,0:T(8,128)S(1)} custom-call(f32[128,256]{1,0:T(8,128)} %bitcast.8, f32[1,64]{1,0:T(1,128)} %bitcast.10, s32[1,1]{1,0:T(1,128)} %bitcast.6.counts_hbm, s32[1,16]{1,0:T(1,128)} %bitcast.11, s32[16,512]{1,0:T(8,128)} %bitcast.9, f32[256,256]{1,0:T(8,128)} %k_hbm.1, f32[256,256]{1,0:T(8,128)} %p_hbm.1), custom_call_target="tpu_custom_call" | custom-call | tf_op jit(solution)/shard_map/pallas_call | solution.py:359
  62.5 0.7 %copy.10 = f32[1,1,1,2,64,256]{5,4,3,2,1,0:T(8,128)} copy(f32[1,1,1,2,64,256]{5,4,3,2,1,0:T(8,128)S(1)} %bitcast.7) | data formatting | bytes 262144
